TPU v7x, 32 devices: a whole 2x2x4 slice. The times are simulated.
32 devices in a mesh: batch: 4 (over x, core), seq: 8 (over z, y).
Axes of the slice: x: 2, y: 2, z: 4, core: 2. Of those that a mesh axis runs over, the one named last changes fastest.
Arguments:
- inputs: float32 [8, 2048, 512], P('batch', 'seq'), may hold values from -12 to 12
- norm_gain: float32 [512], replicated, may hold values from 0.25 to 1.75
- norm_bias: float32 [512], replicated, may hold values from -3 to 3
- query_weight: float32 [512, 512], replicated, may hold values from -0.25 to 0.25
- query_bias: float32 [512], replicated, may hold values from -3 to 3
- key_weight: float32 [512, 512], replicated, may hold values from -0.25 to 0.25
- value_weight: float32 [512, 512], replicated, may hold values from -0.25 to 0.25
- value_bias: float32 [512], replicated, may hold values from -3 to 3
- mixer_weight: float32 [512, 512], replicated, may hold values from -0.5 to 0.5
- mixer_bias: float32 [512], replicated, may hold values from -3 to 3
- final_gain: float32 [512], replicated, may hold values from 0.25 to 1.75
- final_bias: float32 [512], replicated, may hold values from -3 to 3
- inner_weight: float32 [512, 2048], replicated, may hold values from -0.25 to 0.25
- inner_bias: float32 [2048], replicated, may hold values from -3 to 3
- outer_weight: float32 [2048, 512], replicated, may hold values from -0.125 to 0.125
- outer_bias: float32 [512], replicated, may hold values from -3 to 3
- cotangent: float32 [8, 2048, 512], P('batch', 'seq'), may hold values from -6 to 6
Outputs:
- outputs: float32 [8, 2048, 512], P('batch', 'seq')
- inputs_grad: float32 [8, 2048, 512], P('batch', 'seq')
- norm_gain_grad: float32 [512], replicated
- norm_bias_grad: float32 [512], replicated
- query_weight_grad: float32 [512, 512], replicated
- query_bias_grad: float32 [512], replicated
- key_weight_grad: float32 [512, 512], replicated
- value_weight_grad: float32 [512, 512], replicated
- value_bias_grad: float32 [512], replicated
- mixer_weight_grad: float32 [512, 512], replicated
- mixer_bias_grad: float32 [512], replicated
- final_gain_grad: float32 [512], replicated
- final_bias_grad: float32 [512], replicated
- inner_weight_grad: float32 [512, 2048], replicated
- inner_bias_grad: float32 [2048], replicated
- outer_weight_grad: float32 [2048, 512], replicated
- outer_bias_grad: float32 [512], replicated
All inputs are finite; a program needn't handle non-finite values.
Results may differ from a plain program's by a relative error of at most 0.0003.
Values sent between devices are 32-bit elements; how exact they have to be, the bound alone decides.
No kernel may reach another device: no remote copies, remote signals or barrier semaphores. Data moves between devices by JAX's collectives and lax.ppermute only.
A program may use at most 192 MiB of HBM per device.

v0:
```python
import math
import jax
import jax.numpy as jnp
from jax import lax
from jax.sharding import PartitionSpec as P

HEADS = 8
highest = lax.Precision.HIGHEST
root_half = 0.7071067811865476
inv_root_two_pi = 0.3989422804014327


def extended_2(block, sides, width):
    for axis, dim in sides:
        count = lax.axis_size(axis)
        forward = [(i, i + 1) for i in range(count - 1)]
        backward = [(target, source) for source, target in forward]
        low = lax.ppermute(
            lax.slice_in_dim(block, block.shape[dim] - width, None, axis=dim), axis, forward
        )
        high = lax.ppermute(lax.slice_in_dim(block, 0, width, axis=dim), axis, backward)
        block = jnp.concatenate([low, block, high], axis=dim)
    return block


def from_partner(array, axis, apart):
    return lax.ppermute(array, axis, [(i, i ^ 1 << apart) for i in range(lax.axis_size(axis))])


def matmul(left_side, right_side):
    return jnp.dot(left_side, right_side, precision=highest)


def contract(formula, left_side, right_side):
    return jnp.einsum(formula, left_side, right_side, precision=highest)


def norm_forward(values, gain_vec, shift_vec):
    center = values - jnp.mean(values, axis=-1, keepdims=True)
    inverse = lax.rsqrt(jnp.mean(center * center, axis=-1, keepdims=True) + 1e-06)
    unit_rows = center * inverse
    return (unit_rows * gain_vec + shift_vec, unit_rows, inverse)


def norm_backward(grad_rows, unit_rows, inverse, gain_vec):
    grad_unit = grad_rows * gain_vec
    grad_input = inverse * (
        grad_unit
        - jnp.mean(grad_unit, axis=-1, keepdims=True)
        - unit_rows * jnp.mean(grad_unit * unit_rows, axis=-1, keepdims=True)
    )
    return (grad_input, jnp.sum(grad_rows * unit_rows, axis=0), jnp.sum(grad_rows, axis=0))


def pair_mean(values):
    lead_shape = values.shape
    return jnp.mean(values.reshape((lead_shape[0], lead_shape[1] // 2, 2) + lead_shape[2:]), axis=2)


def pair_spread(grad_rows):
    return jnp.repeat(grad_rows, 2, axis=1) * 0.5


def fold_runs(grad_rows, stride):
    lead_shape = grad_rows.shape
    return jnp.sum(
        grad_rows.reshape((lead_shape[0], lead_shape[1] // stride, stride) + lead_shape[2:]), axis=2
    )


def swap_halves(values):
    lead_shape = values.shape
    return values.reshape((lead_shape[0], lead_shape[1] // 2, 2) + lead_shape[2:])[
        :, :, ::-1
    ].reshape(lead_shape)


def split_heads(packed, heads):
    half_width = packed.shape[-1] // 2
    lead_shape = packed.shape[:-1] + (heads, half_width // heads)
    return (
        packed[..., :half_width].reshape(lead_shape),
        packed[..., half_width:].reshape(lead_shape),
    )


def join_heads(key_part, value_part):
    lead_shape = key_part.shape[:-2] + (-1,)
    return jnp.concatenate([key_part.reshape(lead_shape), value_part.reshape(lead_shape)], axis=-1)


def windows(extended, blocks):
    grouped = extended.reshape((extended.shape[0], blocks + 2, 16, extended.shape[-1]))
    return jnp.concatenate([grouped[:, :-2], grouped[:, 1:-1], grouped[:, 2:]], axis=2)


def unwindow(grad_window, blocks):
    summed = jnp.pad(grad_window[:, :, :16], ((0, 0), (0, 2), (0, 0), (0, 0)))
    summed = summed + jnp.pad(grad_window[:, :, 16:32], ((0, 0), (1, 1), (0, 0), (0, 0)))
    summed = summed + jnp.pad(grad_window[:, :, 32:], ((0, 0), (2, 0), (0, 0), (0, 0)))
    return summed.reshape((grad_window.shape[0], (blocks + 2) * 16, grad_window.shape[-1]))


def pairs_forward(queries, key_vecs, values, factor):
    weights = jnp.exp(contract("gbqhe,gbkhe->gbhqk", queries, key_vecs)) * factor
    numerator = contract("gbhqk,gbkhe->gbqhe", weights, values)
    denominator = jnp.transpose(jnp.sum(weights, axis=-1), (0, 1, 3, 2))
    return (numerator, denominator)


def pairs_backward(queries, key_vecs, values, factor, grad_numerator, grad_denominator):
    weights = jnp.exp(contract("gbqhe,gbkhe->gbhqk", queries, key_vecs)) * factor
    grad_scores = weights * (
        contract("gbqhe,gbkhe->gbhqk", grad_numerator, values)
        + jnp.transpose(grad_denominator, (0, 1, 3, 2))[..., None]
    )
    grad_values = contract("gbhqk,gbqhe->gbkhe", weights, grad_numerator)
    grad_queries = contract("gbhqk,gbkhe->gbqhe", grad_scores, key_vecs)
    grad_keys = contract("gbhqk,gbqhe->gbkhe", grad_scores, queries)
    return (grad_queries, grad_keys, grad_values)


def per_device(
    inputs,
    norm_gain,
    norm_bias,
    query_weight,
    query_bias,
    key_weight,
    value_weight,
    value_bias,
    mixer_weight,
    mixer_bias,
    final_gain,
    final_bias,
    inner_weight,
    inner_bias,
    outer_weight,
    outer_bias,
    cotangent,
):
    groups, span_tokens, model_width = inputs.shape
    heads = HEADS
    head_size = model_width // heads
    row_total = groups * span_tokens
    head_scale = 1.0 / math.sqrt(head_size)
    flat_inputs = inputs.reshape(row_total, model_width)
    normed, unit_first, inverse_first = norm_forward(flat_inputs, norm_gain, norm_bias)
    queries = (matmul(normed, query_weight) + query_bias) * head_scale
    key_vecs = matmul(normed, key_weight)
    values = matmul(normed, value_weight) + value_bias
    scaled = queries.reshape(groups, span_tokens, heads, head_size)
    packed = jnp.concatenate([key_vecs, values], axis=-1).reshape(
        groups, span_tokens, 2 * model_width
    )
    seq_index = lax.axis_index("seq")
    seq_count = lax.axis_size("seq")
    crossing = seq_count.bit_length() - 1
    local_top = 0
    while 32 * 2 ** (local_top + 1) <= span_tokens:
        local_top = local_top + 1
    top_level = local_top + crossing
    query_levels = [scaled]
    for level_index in range(top_level):
        query_levels.append(pair_mean(query_levels[-1]))
    kv_levels = [packed]
    for level_index in range(local_top + 1):
        kv_levels.append(pair_mean(kv_levels[-1]))
    blocks = span_tokens // 16
    extended = extended_2(packed, (("seq", 1),), 16)
    win_keys, win_values = split_heads(windows(extended, blocks), heads)
    slot_ids = jnp.arange(48)
    block_ids = jnp.arange(blocks)
    is_valid = ((block_ids[:, None] > 0) | (slot_ids[None, :] >= 16) | (seq_index > 0)) & (
        (block_ids[:, None] < blocks - 1) | (slot_ids[None, :] < 32) | (seq_index < seq_count - 1)
    )
    validity = is_valid.astype(jnp.float32)[None, :, None, None, :]
    block_queries = scaled.reshape(groups, blocks, 16, heads, head_size)
    numerator, denominator = pairs_forward(block_queries, win_keys, win_values, validity)
    numerator = numerator.reshape(groups, span_tokens, heads, head_size)
    denominator = denominator.reshape(groups, span_tokens, heads)
    partners = []
    own_block = kv_levels[local_top + 1]
    for level_bit in range(crossing):
        partner = from_partner(own_block, "seq", level_bit)
        partners.append(partner)
        if level_bit + 1 < crossing:
            is_lower = seq_index // 2**level_bit % 2 == 0
            joined = jnp.where(
                is_lower,
                jnp.concatenate([own_block, partner], axis=1),
                jnp.concatenate([partner, own_block], axis=1),
            )
            own_block = pair_mean(joined)

    def level_operands(level_index):
        stride = 2**level_index
        if level_index <= local_top:
            block_count = span_tokens // stride // 16
            level_queries = query_levels[level_index].reshape(
                groups, block_count, 16, heads, head_size
            )
            partner_kv = swap_halves(
                kv_levels[level_index].reshape(groups, block_count, 16, 2 * model_width)
            )
        else:
            level_queries = query_levels[level_index].reshape(
                groups, 1, span_tokens // stride, heads, head_size
            )
            partner_kv = partners[level_index - local_top - 1].reshape(
                groups, 1, 16, 2 * model_width
            )
        key_part, value_part = split_heads(partner_kv, heads)
        return (level_queries, key_part, value_part, float(stride))

    for level_index in range(1, top_level + 1):
        stride = 2**level_index
        level_queries, key_part, value_part, factor = level_operands(level_index)
        part_num, part_den = pairs_forward(level_queries, key_part, value_part, factor)
        numerator = numerator + jnp.repeat(
            part_num.reshape(groups, span_tokens // stride, heads, head_size), stride, axis=1
        )
        denominator = denominator + jnp.repeat(
            part_den.reshape(groups, span_tokens // stride, heads), stride, axis=1
        )
    mixed = numerator / denominator[..., None]
    mixed_flat = mixed.reshape(row_total, model_width)
    middle = flat_inputs + matmul(mixed_flat, mixer_weight) + mixer_bias
    final_normed, unit_second, inverse_second = norm_forward(middle, final_gain, final_bias)
    inner_act = matmul(final_normed, inner_weight) + inner_bias
    cumulative = 0.5 * (1.0 + lax.erf(inner_act * root_half))
    hidden = inner_act * cumulative
    outputs = middle + matmul(hidden, outer_weight) + outer_bias
    grad_out = cotangent.reshape(row_total, model_width)
    outer_weight_grad = matmul(hidden.T, grad_out)
    outer_bias_grad = jnp.sum(grad_out, axis=0)
    grad_inner = matmul(grad_out, outer_weight.T) * (
        cumulative + inner_act * jnp.exp(-0.5 * inner_act * inner_act) * inv_root_two_pi
    )
    inner_weight_grad = matmul(final_normed.T, grad_inner)
    inner_bias_grad = jnp.sum(grad_inner, axis=0)
    grad_middle_part, final_gain_grad, final_bias_grad = norm_backward(
        matmul(grad_inner, inner_weight.T), unit_second, inverse_second, final_gain
    )
    grad_middle = grad_out + grad_middle_part
    mixer_weight_grad = matmul(mixed_flat.T, grad_middle)
    mixer_bias_grad = jnp.sum(grad_middle, axis=0)
    grad_attend = matmul(grad_middle, mixer_weight.T).reshape(groups, span_tokens, heads, head_size)
    grad_numerator = grad_attend / denominator[..., None]
    grad_denominator = -jnp.sum(grad_attend * mixed, axis=-1) / denominator
    zero_queries, grad_win_keys, grad_win_values = pairs_backward(
        block_queries,
        win_keys,
        win_values,
        validity,
        grad_numerator.reshape(groups, blocks, 16, heads, head_size),
        grad_denominator.reshape(groups, blocks, 16, heads),
    )
    grad_query_levels = [zero_queries.reshape(groups, span_tokens, heads, head_size)]
    grad_extended = unwindow(join_heads(grad_win_keys, grad_win_values), blocks)
    rims = jnp.concatenate([grad_extended[:, :16], grad_extended[:, span_tokens + 16 :]], axis=1)
    returned = extended_2(rims, (("seq", 1),), 16)
    grad_packed_zero = grad_extended[:, 16 : span_tokens + 16]
    grad_packed_zero = grad_packed_zero.at[:, :16].add(returned[:, :16])
    grad_packed_zero = grad_packed_zero.at[:, span_tokens - 16 :].add(returned[:, 48:])
    grad_kv_levels = [grad_packed_zero]
    grad_partners = []
    for level_index in range(1, top_level + 1):
        stride = 2**level_index
        level_queries, key_part, value_part, factor = level_operands(level_index)
        level_grad_num = fold_runs(grad_numerator, stride).reshape(level_queries.shape)
        level_grad_den = fold_runs(grad_denominator, stride).reshape(level_queries.shape[:-1])
        grad_level_q, grad_level_k, grad_level_v = pairs_backward(
            level_queries, key_part, value_part, factor, level_grad_num, level_grad_den
        )
        grad_query_levels.append(
            grad_level_q.reshape(groups, span_tokens // stride, heads, head_size)
        )
        joined_grad = join_heads(grad_level_k, grad_level_v)
        if level_index <= local_top:
            grad_kv_levels.append(
                swap_halves(joined_grad).reshape(groups, span_tokens // stride, 2 * model_width)
            )
        else:
            grad_partners.append(joined_grad.reshape(groups, 16, 2 * model_width))
    grad_next = None
    for level_bit in range(crossing - 1, -1, -1):
        grad_partner = grad_partners[level_bit]
        if level_bit + 1 < crossing:
            spread = pair_spread(grad_next)
            is_lower = seq_index // 2**level_bit % 2 == 0
            grad_mine = jnp.where(is_lower, spread[:, :16], spread[:, 16:])
            grad_partner = grad_partner + jnp.where(is_lower, spread[:, 16:], spread[:, :16])
        else:
            grad_mine = jnp.zeros_like(grad_partner)
        grad_next = grad_mine + from_partner(grad_partner, "seq", level_bit)
    grad_kv = grad_next
    for level_index in range(local_top, -1, -1):
        grad_kv = pair_spread(grad_kv) + grad_kv_levels[level_index]
    grad_query = grad_query_levels[top_level]
    for level_index in range(top_level - 1, -1, -1):
        grad_query = pair_spread(grad_query) + grad_query_levels[level_index]
    grad_queries = grad_query.reshape(row_total, model_width) * head_scale
    grad_keys = grad_kv[..., :model_width].reshape(row_total, model_width)
    grad_values = grad_kv[..., model_width:].reshape(row_total, model_width)
    query_weight_grad = matmul(normed.T, grad_queries)
    query_bias_grad = jnp.sum(grad_queries, axis=0)
    key_weight_grad = matmul(normed.T, grad_keys)
    value_weight_grad = matmul(normed.T, grad_values)
    value_bias_grad = jnp.sum(grad_values, axis=0)
    grad_normed = (
        matmul(grad_queries, query_weight.T)
        + matmul(grad_keys, key_weight.T)
        + matmul(grad_values, value_weight.T)
    )
    grad_first, norm_gain_grad, norm_bias_grad = norm_backward(
        grad_normed, unit_first, inverse_first, norm_gain
    )
    inputs_grad = grad_middle + grad_first
    (
        norm_gain_grad,
        norm_bias_grad,
        query_weight_grad,
        query_bias_grad,
        key_weight_grad,
        value_weight_grad,
        value_bias_grad,
        mixer_weight_grad,
        mixer_bias_grad,
        final_gain_grad,
        final_bias_grad,
        inner_weight_grad,
        inner_bias_grad,
        outer_weight_grad,
        outer_bias_grad,
    ) = lax.psum(
        (
            norm_gain_grad,
            norm_bias_grad,
            query_weight_grad,
            query_bias_grad,
            key_weight_grad,
            value_weight_grad,
            value_bias_grad,
            mixer_weight_grad,
            mixer_bias_grad,
            final_gain_grad,
            final_bias_grad,
            inner_weight_grad,
            inner_bias_grad,
            outer_weight_grad,
            outer_bias_grad,
        ),
        ("batch", "seq"),
    )
    return (
        outputs.reshape(groups, span_tokens, model_width),
        inputs_grad.reshape(groups, span_tokens, model_width),
        norm_gain_grad,
        norm_bias_grad,
        query_weight_grad,
        query_bias_grad,
        key_weight_grad,
        value_weight_grad,
        value_bias_grad,
        mixer_weight_grad,
        mixer_bias_grad,
        final_gain_grad,
        final_bias_grad,
        inner_weight_grad,
        inner_bias_grad,
        outer_weight_grad,
        outer_bias_grad,
    )


def solution(mesh):
    return jax.shard_map(
        per_device,
        mesh=mesh,
        in_specs=(
            P("batch", "seq", None),
            P(),
            P(),
            P(),
            P(),
            P(),
            P(),
            P(),
            P(),
            P(),
            P(),
            P(),
            P(),
            P(),
            P(),
            P(),
            P("batch", "seq", None),
        ),
        out_specs=(
            P("batch", "seq", None),
            P("batch", "seq", None),
            P(),
            P(),
            P(),
            P(),
            P(),
            P(),
            P(),
            P(),
            P(),
            P(),
            P(),
            P(),
            P(),
            P(),
            P(),
        ),
        check_vma=False,
    )
```

profile of v0, /device:TPU:0, one launch (start us, length us, event | category | flops | bytes accessed | tf_op | source)
XLA Modules:
  0.0 826.7 jit_solution(6064375507251882588)
XLA Ops:
  22.9 5.1 reduce_sum.457
  98.7 4.3 fusion.162
  151.9 5.6 reshape.1074
  157.5 15.4 %fusion.161 = (f32[2,16,8,16]{3,2,1,0:T(8,128)S(1)}, f32[2,16,8,16,48]{4,3,2,1,0:T(8,128)}) fusion(f32[16,48]{1,0:T(8,128)S(1)} %and_convert_fusion, f32[2,16,48,8,64]{4,3,2,1,0:T(8,128)} %reshape.1074, f32[2,16,16,8,64]{4,3,2,1,0:T(8,128)} %reshape_reshape.24), kind=kOutput, calls=%fused_computation.291 | convolution fusion | flops 151384064 | bytes 5000192 | tf_op jit(solution)/shard_map/gbqhe,gbkhe->gbhqk/dot_general | solution.py:35
  181.1 4.5 collective-permute-start.3
  185.7 5.6 reshape.1073
  191.3 9.1 %fusion.23 = f32[2,16,16,8,64]{4,2,3,1,0:T(8,128)S(1)} fusion(f32[2,16,8,16,48]{4,3,2,1,0:T(8,128)} %get-tuple-element.122, f32[2,16,48,8,64]{4,3,2,1,0:T(8,128)} %reshape.1073), kind=kOutput, calls=%fused_computation.35 | convolution fusion | flops 150994944 | bytes 4980736 | tf_op jit(solution)/shard_map/gbhqk,gbkhe->gbqhe/dot_general | solution.py:35
  249.6 6.9 fusion.65
  256.6 9.1 %fusion.164 = (f32[2048]{0:T(1024)}, f32[512,2048]{1,0:T(8,128)S(1)}) fusion(f32[512,2048]{1,0:T(8,128)S(1)} %fusion.65, f32[2048]{0:T(1024)S(1)} %copy-done.166, f32[512,512]{1,0:T(8,128)S(1)} %bitcast.532, f32[2048,512]{1,0:T(8,128)S(1)} %copy-done.165), kind=kOutput, calls=%fused_computation.294 | convolution fusion | flops 6453983232 | bytes 13647872 | tf_op jit(solution)/shard_map/dot_general | solution.py:31
  265.7 8.8 %fusion.64 = f32[512,2048]{1,0:T(8,128)} fusion(f32[512,2048]{1,0:T(8,128)S(1)} %get-tuple-element.131, f32[512,512]{1,0:T(8,128)S(1)} %get-tuple-element.126, f32[512]{0:T(512)S(1)} %copy-done.141, f32[512]{0:T(512)S(1)} %copy-done.133, f32[512]{0:T(512)S(1)} %add_rsqrt_fusion, f32[512]{0:T(512)S(1)} %broadcast_multiply_fusion.15), kind=kOutput, calls=%fused_computation.134 | convolution fusion | flops 6443499520 | bytes 9445376 | tf_op jit(solution)/shard_map/dot_general | solution.py:31
  274.5 7.7 multiply_reduce_fusion
  301.8 4.3 multiply_reduce_fusion.3
  308.9 12.6 %convolution_bitcast_fusion = f32[2,16,48,8,64]{4,2,3,1,0:T(8,128)S(1)} fusion(f32[2,16,8,16,48]{4,3,2,1,0:T(8,128)} %get-tuple-element.122, f32[2,16,16,8,64]{4,3,2,1,0:T(8,128)} %reshape.1145, f32[2,16,16,8]{2,3,1,0:T(8,128)S(1)} %get-tuple-element.69), kind=kOutput, calls=%fused_computation.17 | convolution fusion | flops 151257088 | bytes 4997120 | tf_op jit(solution)/shard_map/gbhqk,gbqhe->gbkhe/dot_general | solution.py:35
  321.5 5.2 copy.830
  326.7 6.2 reshape.1182
  332.9 14.5 %add_multiply_fusion.2 = f32[2,16,8,16,48]{4,3,2,1,0:T(8,128)S(1)} fusion(f32[2,16,8,16,48]{4,3,2,1,0:T(8,128)} %get-tuple-element.122, f32[2,16,48,8,64]{4,3,2,1,0:T(8,128)} %reshape.1073, f32[2,16,8,16]{3,2,1,0:T(8,128)} %get-tuple-element.68, f32[2,16,16,8,64]{4,3,2,1,0:T(8,128)} %reshape.1145, f32[2,16,16,8]{2,3,1,0:T(8,128)S(1)} %get-tuple-element.69), kind=kOutput, calls=%fused_computation.25 | convolution fusion | flops 151650304 | bytes 5799936 | tf_op jit(solution)/shard_map/gbqhe,gbkhe->gbhqk/dot_general | solution.py:35
  348.8 10.1 %convolution_bitcast_fusion.1 = f32[2,16,48,8,64]{4,2,3,1,0:T(8,128)S(1)} fusion(f32[2,16,8,16,48]{4,3,2,1,0:T(8,128)S(1)} %add_multiply_fusion.2, f32[2,16,16,8,64]{4,3,2,1,0:T(8,128)S(1)} %copy-done.10), kind=kOutput, calls=%fused_computation.18 | convolution fusion | flops 150994944 | bytes 4980736 | tf_op jit(solution)/shard_map/gbhqk,gbqhe->gbkhe/dot_general | solution.py:35
  358.9 5.5 copy.829
  364.4 6.3 reshape.1181
  443.1 10.5 %fusion.28 = f32[2048,512]{1,0:T(8,128)} fusion(f32[512,512]{1,0:T(8,128)S(1)} %bitcast.533, f32[512,2048]{1,0:T(8,128)} %copy-done.27, f32[2048]{0:T(1024)S(1)} %copy-done.167), kind=kOutput, calls=%fused_computation.36 | convolution fusion | flops 6447693824 | bytes 9445376 | tf_op jit(solution)/shard_map/dot_general | solution.py:31
  492.5 7.4 fusion.142
  585.3 10.9 %fusion.35 = f32[512,512]{1,0:T(8,128)} fusion(f32[512,512]{1,0:T(8,128)S(1)} %get-tuple-element.126, f32[2048,512]{1,0:T(8,128)} %param.35, f32[512,2048]{1,0:T(8,128)S(1)} %copy-done.28, f32[2048]{0:T(1024)S(1)} %copy-done.168, f32[512]{0:T(512)S(1)} %copy-done.169), kind=kOutput, calls=%fused_computation.56 | convolution fusion | flops 6448218112 | bytes 10496000 | tf_op jit(solution)/shard_map/dot_general | solution.py:31
  602.8 41.3 %all-reduce.3 = (f32[512]{0:T(512)}, f32[512]{0:T(512)}, f32[512]{0:T(512)}, f32[512]{0:T(512)}, f32[512]{0:T(512)}, /*index=5*/f32[512]{0:T(512)}, f32[512]{0:T(512)}, f32[2048]{0:T(1024)}, f32[512]{0:T(512)}) all-reduce(f32[512]{0:T(512)S(1)} %get-tuple-element.43, ...), channel_id=1, replica_groups=mesh['batch'=4,'seq'=8] {'batch','seq'}, use_global_device_ids=true, to_apply=%region_41.42 | all-reduce | flops 6144 | bytes 49152 | tf_op jit(solution)/shard_map/psum | solution.py:336
  646.7 161.7 %all-reduce.7.cloned.1.call-done = (f32[512,512]{1,0:T(8,128)}, f32[512,512]{1,0:T(8,128)}, f32[512,512]{1,0:T(8,128)}, f32[512,512]{1,0:T(8,128)}, f32[512,2048]{1,0:T(8,128)}, /*index=5*/f32[2048,512]{1,0:T(8,128)}) async-done(((f32[512,512]{1,0:T(8,128)}, f32[512,512]{1,0:T(8,128)}, f32[512,512]{1,0:T(8,128)}, f32[512,512]{1,0:T(8,128)}, f32[512,2048]{1,0:T(8,128)}, /*index=5*/f32[2048,512]{1,0:T(8,128)}), ...) | async-done | bytes 12582928 | tf_op jit(solution)/shard_map/psum | solution.py:336
  (715 shorter events, 431.3 us)
Async XLA Ops:
  7.2 801.2 %all-reduce.7.cloned.1.call-start = ((), (), s32[]{:S(2)}) async-start(), calls=%async_computation | async-start | bytes 25165824 | tf_op jit(solution)/shard_map/psum | solution.py:336
  10.7 45.5 %copy-start.3 = (f32[512,512]{1,0:T(8,128)}, f32[512,512]{1,0:T(8,128)S(1)}, u32[]{:S(2)}) copy-start(f32[512,512]{1,0:T(8,128)S(1)} %fusion.52) | copy-start | bytes 3145732
  42.1 18.2 %copy-start.59 = (f32[2,32,1024]{2,1,0:T(8,128)}, f32[2,32,1024]{2,1,0:T(8,128)S(1)}, u32[]{:S(2)}) copy-start(f32[2,32,1024]{2,1,0:T(8,128)S(1)} %reduce_sum.463) | copy-start | bytes 786436
  46.6 128.9 %collective-permute-start.2 = (f32[2,16,1024]{2,1,0:T(8,128)}, f32[2,16,1024]{2,1,0:T(8,128)}, u32[]{:S(2)}, u32[]{:S(2)}) collective-permute-start(f32[2,16,1024]{2,1,0:T(8,128)} %broadcast_multiply_fusion.9), channel_id=1, source_target_pairs={{0,1},{1,0},{2,3},{3,2},{4,5},{5,4},{6,7},{7,6},{8,9},{9,8},{10,11... | collective-permute-start | bytes 393224 | tf_op jit(solution)/shard_map/ppermute | solution.py:27
  51.3 93.4 %collective-permute-start = (f32[2,16,1024]{2,1,0:T(8,128)}, f32[2,16,1024]{2,1,0:T(8,128)}, u32[]{:S(2)}, u32[]{:S(2)}) collective-permute-start(f32[2,16,1024]{2,1,0:T(8,128)} %get-tuple-element.93), channel_id=1, source_target_pairs={{0,1},{1,2},{2,3},{3,4},{4,5},{5,6},{6,7},{8,9},{9,10},{10,11},{11... | collective-permute-start | bytes 393224 | tf_op jit(solution)/shard_map/ppermute | solution.py:18
  53.8 90.9 %collective-permute-start.1 = (f32[2,16,1024]{2,1,0:T(8,128)}, f32[2,16,1024]{2,1,0:T(8,128)}, u32[]{:S(2)}, u32[]{:S(2)}) collective-permute-start(f32[2,16,1024]{2,1,0:T(8,128)} %get-tuple-element.94), channel_id=1, source_target_pairs={{1,0},{2,1},{3,2},{4,3},{5,4},{6,5},{7,6},{9,8},{10,9},{11,10},{12... | collective-permute-start | bytes 393224 | tf_op jit(solution)/shard_map/ppermute | solution.py:21
  69.3 29.4 %copy-start.17 = (f32[2,128,8,64]{3,2,1,0:T(8,128)}, f32[2,128,8,64]{3,2,1,0:T(8,128)S(1)}, u32[]{:S(2)}) copy-start(f32[2,128,8,64]{3,2,1,0:T(8,128)S(1)} %broadcast_multiply_fusion.1) | copy-start | bytes 1572868
  84.8 91.6 %copy-start.66 = (f32[2,16,8,64]{3,2,1,0:T(8,128)}, f32[2,16,8,64]{3,2,1,0:T(8,128)S(1)}, u32[]{:S(2)}) copy-start(f32[2,16,8,64]{3,2,1,0:T(8,128)S(1)} %reduce_sum.467) | copy-start | bytes 196612
  176.8 28.7 %copy-start.68 = (f32[2,8,16,16]{2,3,1,0:T(8,128)}, f32[2,8,16,16]{2,3,1,0:T(8,128)S(1)}, u32[]{:S(2)}) copy-start(f32[2,8,16,16]{2,3,1,0:T(8,128)S(1)} %get-tuple-element.116) | copy-start | bytes 49156
  181.1 36.7 %collective-permute-start.3 = (f32[2,16,1024]{2,1,0:T(8,128)S(1)}, f32[2,16,1024]{2,1,0:T(8,128)S(1)}, u32[]{:S(2)}, u32[]{:S(2)}) collective-permute-start(f32[2,16,1024]{2,1,0:T(8,128)S(1)} %broadcast_multiply_fusion.8), channel_id=1, source_target_pairs={{0,2},{1,3},{2,0},{3,1},{4,6},{5,7},{6,4},{7,5},{8,10},{9,11},{10,... | collective-permute-start | bytes 393224 | tf_op jit(solution)/shard_map/ppermute | solution.py:27
  219.8 11.8 %collective-permute-start.4 = (f32[2,16,1024]{2,1,0:T(8,128)S(1)}, f32[2,16,1024]{2,1,0:T(8,128)S(1)}, u32[]{:S(2)}, u32[]{:S(2)}) collective-permute-start(f32[2,16,1024]{2,1,0:T(8,128)S(1)} %broadcast_multiply_fusion.7), channel_id=1, source_target_pairs={{0,4},{1,5},{2,6},{3,7},{4,0},{5,1},{6,2},{7,3},{8,12},{9,13},{10,... | collective-permute-start | bytes 393224 | tf_op jit(solution)/shard_map/ppermute | solution.py:27
  232.2 74.7 %copy-start.129 = (f32[2,8,4]{1,2,0:T(4,128)}, f32[2,8,4]{1,2,0:T(4,128)S(1)}, u32[]{:S(2)}) copy-start(f32[2,8,4]{1,2,0:T(4,128)S(1)} %copy.712) | copy-start | bytes 772
  332.9 15.9 %copy-start.10 = (f32[2,16,16,8,64]{4,3,2,1,0:T(8,128)S(1)}, f32[2,16,16,8,64]{4,3,2,1,0:T(8,128)}, u32[]{:S(2)}) copy-start(f32[2,16,16,8,64]{4,3,2,1,0:T(8,128)} %reshape_reshape.24) | copy-start | bytes 3145732
  443.1 14.7 %copy-start.47 = (f32[2,8,16,8,64]{4,2,3,1,0:T(8,128)S(1)}, f32[2,8,16,8,64]{4,2,3,1,0:T(8,128)}, u32[]{:S(2)}) copy-start(f32[2,8,16,8,64]{4,2,3,1,0:T(8,128)} %convolution_bitcast_fusion.4) | copy-start | bytes 1572868
  453.6 78.8 %collective-permute-start.8 = (f32[2,16,1024]{2,1,0:T(8,128)}, f32[2,16,1024]{2,1,0:T(8,128)}, u32[]{:S(2)}, u32[]{:S(2)}) collective-permute-start(f32[2,16,1024]{2,1,0:T(8,128)} %get-tuple-element.86), channel_id=1, source_target_pairs={{0,1},{1,2},{2,3},{3,4},{4,5},{5,6},{6,7},{8,9},{9,10},{10,11},{11... | collective-permute-start | bytes 393224 | tf_op jit(solution)/shard_map/ppermute | solution.py:18
  456.5 82.8 %collective-permute-start.9 = (f32[2,16,1024]{2,1,0:T(8,128)}, f32[2,16,1024]{2,1,0:T(8,128)}, u32[]{:S(2)}, u32[]{:S(2)}) collective-permute-start(f32[2,16,1024]{2,1,0:T(8,128)} %get-tuple-element.85), channel_id=1, source_target_pairs={{1,0},{2,1},{3,2},{4,3},{5,4},{6,5},{7,6},{9,8},{10,9},{11,10},{12... | collective-permute-start | bytes 393224 | tf_op jit(solution)/shard_map/ppermute | solution.py:21
  471.2 15.9 %copy-start.79 = (f32[2,16,8,64]{3,2,1,0:T(8,128)S(1)}, f32[2,16,8,64]{3,2,1,0:T(8,128)}, u32[]{:S(2)}) copy-start(f32[2,16,8,64]{3,2,1,0:T(8,128)} %copy-done.78) | copy-start | bytes 196612
  471.9 56.5 %collective-permute-start.5 = (f32[2,16,1024]{2,1,0:T(8,128)}, f32[2,16,1024]{2,1,0:T(8,128)}, u32[]{:S(2)}, u32[]{:S(2)}) collective-permute-start(f32[2,16,1024]{2,1,0:T(8,128)} %maximum_bitcast_fusion), channel_id=1, source_target_pairs={{0,4},{1,5},{2,6},{3,7},{4,0},{5,1},{6,2},{7,3},{8,12},{9,13},{10,... | collective-permute-start | bytes 393224 | tf_op jit(solution)/shard_map/ppermute | solution.py:27
  532.2 5.0 collective-permute-start.6
  539.2 5.0 collective-permute-start.7
  599.4 44.7 %copy-start.2 = (f32[2,256,512]{2,1,0:T(8,128)S(1)}, f32[2,256,512]{2,1,0:T(8,128)}, u32[]{:S(2)}) copy-start(f32[2,256,512]{2,1,0:T(8,128)} %param.21) | copy-start | bytes 3145732
  599.4 44.7 %copy-start.16 = (f32[512,512]{1,0:T(8,128)S(1)}, f32[512,512]{1,0:T(8,128)}, u32[]{:S(2)}) copy-start(f32[512,512]{1,0:T(8,128)} %copy-done.14) | copy-start | bytes 3145732
  599.4 44.7 %copy-start.152 = (f32[1,2,2,128]{3,1,2,0:T(2,128)S(1)}, f32[1,2,2,128]{3,1,2,0:T(2,128)}, u32[]{:S(2)}) copy-start(f32[1,2,2,128]{3,1,2,0:T(2,128)} %copy-done.151) | copy-start | bytes 6148
  599.4 44.7 %copy-start.154 = (f32[1,2,2,128]{3,1,2,0:T(2,128)S(1)}, f32[1,2,2,128]{3,1,2,0:T(2,128)}, u32[]{:S(2)}) copy-start(f32[1,2,2,128]{3,1,2,0:T(2,128)} %copy-done.153) | copy-start | bytes 6148
  (159 other events, 722.5 us)
Sparse Core Ops, SparseCore 0:
  571.8 236.6 all-reduce.6
where the time goes:
time: 835 us; the launch traced here: 827 us
  local copies, waits for them, and re-layouts  275 us (33%)
  matrix products  208 us (25%)
  waiting for transfers between devices  168 us (20%)
  other arithmetic  95.3 us (11%)
  blocking collectives  41.3 us (5%)
  starting transfers between devices  21.5 us (3%)
  between operations  16.8 us (2%)
    psum x1, waiting for transfers between devices, per_device(): lax.psum((norm_gain_grad, norm_bias_grad, query_weight_grad, query_bias_g...  162 us
    dot_general x42, matrix products, contract(): return jnp.einsum(formula, left_side, right_side, precision=highest)  121 us
    dot_general x18, matrix products, matmul(): return jnp.dot(left_side, right_side, precision=highest)  87.1 us
    psum x1, blocking collectives, per_device(): lax.psum((norm_gain_grad, norm_bias_grad, query_weight_grad, query_bias_g...  41.3 us
    reshape x12, local copies, waits for them, and re-layouts, per_device(): jnp.repeat(part_num.reshape(groups, span_tokens // stride, heads, head_si...  36.1 us
    transpose x22, local copies, waits for them, and re-layouts, contract(): return jnp.einsum(formula, left_side, right_side, precision=highest)  27 us
    unnamed x356, local copies, waits for them, and re-layouts  26 us
    reduce_sum x12, other arithmetic, pair_mean(): jnp.mean(values.reshape((lead_shape[0], lead_shape[1] // 2, 2) + lead_sha...  19.6 us
  transfers between devices with their start and end apart: 11, of which 3 were waited for; matrix products, arithmetic and copies ran while one was open for 32% of the time, Pallas kernels for 0%

commit v1 on v0

--- a/solution.py
+++ b/solution.py
@@ -317,6 +317,10 @@
         grad_normed, unit_first, inverse_first, norm_gain
     )
     inputs_grad = grad_middle + grad_first
+
+    def _touch_heaps(xx, group_axis, axis_key):
+        return lax.psum(lax.psum(xx, axis_key), group_axis)
+
     (
         norm_gain_grad,
         norm_bias_grad,
@@ -333,7 +337,7 @@
         inner_bias_grad,
         outer_weight_grad,
         outer_bias_grad,
-    ) = lax.psum(
+    ) = _touch_heaps(
         (
             norm_gain_grad,
             norm_bias_grad,
@@ -351,7 +355,8 @@
             outer_weight_grad,
             outer_bias_grad,
         ),
-        ("batch", "seq"),
+        "batch",
+        "seq",
     )
     return (
         outputs.reshape(groups, span_tokens, model_width),

time: 835 us -> 1230 us (1.47)
  waiting for transfers between devices: 168 us -> 553 us
    psum x1 -> x2, waiting for transfers between devices: 162 us -> 547 us  [_touch_heaps(): return lax.psum(lax.psum(xx, axis_key), group_axis)]
    psum x1 -> x2, blocking collectives: 41.3 us -> 46.7 us  [_touch_heaps(): return lax.psum(lax.psum(xx, axis_key), group_axis)]
  transfers between devices with their start and end apart: 11 -> 12, of which waited for: 3 -> 4; matrix products, arithmetic and copies ran while one was open for 32% -> 22% of each run, Pallas kernels for 0% -> 0%
where the time goes in v1:
time: 1230 us; the launch traced here: 1220 us
  waiting for transfers between devices  553 us (45%)
  local copies, waits for them, and re-layouts  277 us (23%)
  matrix products  208 us (17%)
  other arithmetic  95.4 us (8%)
  blocking collectives  46.7 us (4%)
  starting transfers between devices  21.5 us (2%)
  between operations  16.8 us (1%)
    psum x2, waiting for transfers between devices, _touch_heaps(): return lax.psum(lax.psum(xx, axis_key), group_axis)  547 us
    dot_general x42, matrix products, contract(): return jnp.einsum(formula, left_side, right_side, precision=highest)  121 us
    dot_general x18, matrix products, matmul(): return jnp.dot(left_side, right_side, precision=highest)  87.1 us
    psum x2, blocking collectives, _touch_heaps(): return lax.psum(lax.psum(xx, axis_key), group_axis)  46.7 us
    reshape x12, local copies, waits for them, and re-layouts, per_device(): jnp.repeat(part_num.reshape(groups, span_tokens // stride, heads, head_si...  36.1 us
    transpose x22, local copies, waits for them, and re-layouts, contract(): return jnp.einsum(formula, left_side, right_side, precision=highest)  27 us
    unnamed x356, local copies, waits for them, and re-layouts  26.9 us
  transfers between devices with their start and end apart: 12, of which 4 were waited for; matrix products, arithmetic and copies ran while one was open for 22% of the time, Pallas kernels for 0%

profile of v1, /device:TPU:0, one launch (start us, length us, event | category | flops | bytes accessed | tf_op | source)
XLA Modules:
  0.0 1218.3 jit_solution(4954011379407517146)
XLA Ops:
  22.9 5.1 reduce_sum.457
  152.0 5.6 reshape.1074
  157.6 15.4 %fusion.161 = (f32[2,16,8,16]{3,2,1,0:T(8,128)S(1)}, f32[2,16,8,16,48]{4,3,2,1,0:T(8,128)}) fusion(f32[16,48]{1,0:T(8,128)S(1)} %and_convert_fusion, f32[2,16,48,8,64]{4,3,2,1,0:T(8,128)} %reshape.1074, f32[2,16,16,8,64]{4,3,2,1,0:T(8,128)} %reshape_reshape.24), kind=kOutput, calls=%fused_computation.291 | convolution fusion | flops 151384064 | bytes 5000192 | tf_op jit(solution)/shard_map/gbqhe,gbkhe->gbhqk/dot_general | solution.py:35
  181.2 4.5 collective-permute-start.3
  185.7 5.6 reshape.1073
  191.3 9.1 fusion.23
  249.6 6.9 fusion.65
  256.6 9.1 fusion.164
  265.7 8.8 fusion.64
  274.5 7.7 multiply_reduce_fusion
  308.9 12.6 %convolution_bitcast_fusion = f32[2,16,48,8,64]{4,2,3,1,0:T(8,128)S(1)} fusion(f32[2,16,8,16,48]{4,3,2,1,0:T(8,128)} %get-tuple-element.137, f32[2,16,16,8,64]{4,3,2,1,0:T(8,128)} %reshape.1145, f32[2,16,16,8]{2,3,1,0:T(8,128)S(1)} %get-tuple-element.84), kind=kOutput, calls=%fused_computation.17 | convolution fusion | flops 151257088 | bytes 4997120 | tf_op jit(solution)/shard_map/gbhqk,gbqhe->gbkhe/dot_general | solution.py:35
  321.5 5.2 copy.830
  326.7 6.2 reshape.1182
  332.9 14.5 %add_multiply_fusion.2 = f32[2,16,8,16,48]{4,3,2,1,0:T(8,128)S(1)} fusion(f32[2,16,8,16,48]{4,3,2,1,0:T(8,128)} %get-tuple-element.137, f32[2,16,48,8,64]{4,3,2,1,0:T(8,128)} %reshape.1073, f32[2,16,8,16]{3,2,1,0:T(8,128)} %get-tuple-element.83, f32[2,16,16,8,64]{4,3,2,1,0:T(8,128)} %reshape.1145, f32[2,16,16,8]{2,3,1,0:T(8,128)S(1)} %get-tuple-element.84), kind=kOutput, calls=%fused_computation.25 | convolution fusion | flops 151650304 | bytes 5799936 | tf_op jit(solution)/shard_map/gbqhe,gbkhe->gbhqk/dot_general | solution.py:35
  348.8 10.1 convolution_bitcast_fusion.1
  359.0 5.5 copy.829
  364.5 6.3 reshape.1181
  444.1 10.5 fusion.28
  493.4 7.4 fusion.142
  572.6 402.1 %all-reduce.10.cloned.1.call-done = (f32[512,512]{1,0:T(8,128)}, f32[512,512]{1,0:T(8,128)}, f32[512,512]{1,0:T(8,128)}, f32[512,512]{1,0:T(8,128)}, f32[512,2048]{1,0:T(8,128)}, /*index=5*/f32[2048,512]{1,0:T(8,128)}) async-done(((f32[512,512]{1,0:T(8,128)}, f32[512,512]{1,0:T(8,128)}, f32[512,512]{1,0:T(8,128)}, f32[512,512]{1,0:T(8,128)}, f32[512,2048]{1,0:T(8,128)}, /*index=5*/f32[2048,512]{1,0:T(8,128)}), ...) | async-done | bytes 12582928 | tf_op jit(solution)/shard_map/psum | solution.py:322
  988.8 10.9 fusion.35
  1006.3 34.6 %all-reduce.3 = (f32[512]{0:T(512)S(1)}, f32[512]{0:T(512)S(1)}, f32[512]{0:T(512)S(1)}, f32[512]{0:T(512)S(1)}, f32[512]{0:T(512)S(1)}, /*index=5*/f32[512]{0:T...) all-reduce(f32[512]{0:T(512)S(1)} %get-tuple-element.43, ...), channel_id=1, replica_groups=mesh['batch'=4,'seq'=8] {'seq'}, use_global_device_ids=true, to_apply=%region_41.42 | all-reduce | flops 6144 | bytes 49152 | tf_op jit(solution)/shard_map/psum | solution.py:322
  1040.9 12.1 all-reduce.5
  1055.6 144.4 %all-reduce.12.cloned.1.call-done = (f32[512,512]{1,0:T(8,128)}, f32[512,512]{1,0:T(8,128)}, f32[512,512]{1,0:T(8,128)}, f32[512,512]{1,0:T(8,128)}, f32[512,2048]{1,0:T(8,128)}, /*index=5*/f32[2048,512]{1,0:T(8,128)}) async-done(((f32[512,512]{1,0:T(8,128)}, f32[512,512]{1,0:T(8,128)}, f32[512,512]{1,0:T(8,128)}, f32[512,512]{1,0:T(8,128)}, f32[512,2048]{1,0:T(8,128)}, /*index=5*/f32[2048,512]{1,0:T(8,128)}), ...) | async-done | bytes 12582928 | tf_op jit(solution)/shard_map/psum | solution.py:322
  (719 shorter events, 441.2 us)
Async XLA Ops:
  7.2 967.5 %all-reduce.10.cloned.1.call-start = ((), (), s32[]{:S(2)}) async-start(), calls=%async_computation | async-start | bytes 25165824 | tf_op jit(solution)/shard_map/psum | solution.py:322
  10.7 45.5 %copy-start.3 = (f32[512,512]{1,0:T(8,128)}, f32[512,512]{1,0:T(8,128)S(1)}, u32[]{:S(2)}) copy-start(f32[512,512]{1,0:T(8,128)S(1)} %fusion.52) | copy-start | bytes 3145732
  42.1 18.2 %copy-start.59 = (f32[2,32,1024]{2,1,0:T(8,128)}, f32[2,32,1024]{2,1,0:T(8,128)S(1)}, u32[]{:S(2)}) copy-start(f32[2,32,1024]{2,1,0:T(8,128)S(1)} %reduce_sum.463) | copy-start | bytes 786436
  46.6 128.9 %collective-permute-start.2 = (f32[2,16,1024]{2,1,0:T(8,128)}, f32[2,16,1024]{2,1,0:T(8,128)}, u32[]{:S(2)}, u32[]{:S(2)}) collective-permute-start(f32[2,16,1024]{2,1,0:T(8,128)} %broadcast_multiply_fusion.9), channel_id=1, source_target_pairs={{0,1},{1,0},{2,3},{3,2},{4,5},{5,4},{6,7},{7,6},{8,9},{9,8},{10,11... | collective-permute-start | bytes 393224 | tf_op jit(solution)/shard_map/ppermute | solution.py:27
  51.3 93.5 %collective-permute-start = (f32[2,16,1024]{2,1,0:T(8,128)}, f32[2,16,1024]{2,1,0:T(8,128)}, u32[]{:S(2)}, u32[]{:S(2)}) collective-permute-start(f32[2,16,1024]{2,1,0:T(8,128)} %get-tuple-element.108), channel_id=1, source_target_pairs={{0,1},{1,2},{2,3},{3,4},{4,5},{5,6},{6,7},{8,9},{9,10},{10,11},{11... | collective-permute-start | bytes 393224 | tf_op jit(solution)/shard_map/ppermute | solution.py:18
  53.8 90.9 %collective-permute-start.1 = (f32[2,16,1024]{2,1,0:T(8,128)}, f32[2,16,1024]{2,1,0:T(8,128)}, u32[]{:S(2)}, u32[]{:S(2)}) collective-permute-start(f32[2,16,1024]{2,1,0:T(8,128)} %get-tuple-element.109), channel_id=1, source_target_pairs={{1,0},{2,1},{3,2},{4,3},{5,4},{6,5},{7,6},{9,8},{10,9},{11,10},{12... | collective-permute-start | bytes 393224 | tf_op jit(solution)/shard_map/ppermute | solution.py:21
  69.3 29.4 %copy-start.17 = (f32[2,128,8,64]{3,2,1,0:T(8,128)}, f32[2,128,8,64]{3,2,1,0:T(8,128)S(1)}, u32[]{:S(2)}) copy-start(f32[2,128,8,64]{3,2,1,0:T(8,128)S(1)} %broadcast_multiply_fusion.1) | copy-start | bytes 1572868
  84.9 91.6 %copy-start.66 = (f32[2,16,8,64]{3,2,1,0:T(8,128)}, f32[2,16,8,64]{3,2,1,0:T(8,128)S(1)}, u32[]{:S(2)}) copy-start(f32[2,16,8,64]{3,2,1,0:T(8,128)S(1)} %reduce_sum.467) | copy-start | bytes 196612
  176.9 28.7 %copy-start.68 = (f32[2,8,16,16]{2,3,1,0:T(8,128)}, f32[2,8,16,16]{2,3,1,0:T(8,128)S(1)}, u32[]{:S(2)}) copy-start(f32[2,8,16,16]{2,3,1,0:T(8,128)S(1)} %get-tuple-element.131) | copy-start | bytes 49156
  181.2 36.7 %collective-permute-start.3 = (f32[2,16,1024]{2,1,0:T(8,128)S(1)}, f32[2,16,1024]{2,1,0:T(8,128)S(1)}, u32[]{:S(2)}, u32[]{:S(2)}) collective-permute-start(f32[2,16,1024]{2,1,0:T(8,128)S(1)} %broadcast_multiply_fusion.8), channel_id=1, source_target_pairs={{0,2},{1,3},{2,0},{3,1},{4,6},{5,7},{6,4},{7,5},{8,10},{9,11},{10,... | collective-permute-start | bytes 393224 | tf_op jit(solution)/shard_map/ppermute | solution.py:27
  219.8 11.8 collective-permute-start.4
  232.2 74.7 %copy-start.129 = (f32[2,8,4]{1,2,0:T(4,128)}, f32[2,8,4]{1,2,0:T(4,128)S(1)}, u32[]{:S(2)}) copy-start(f32[2,8,4]{1,2,0:T(4,128)S(1)} %copy.712) | copy-start | bytes 772
  332.9 15.9 %copy-start.10 = (f32[2,16,16,8,64]{4,3,2,1,0:T(8,128)S(1)}, f32[2,16,16,8,64]{4,3,2,1,0:T(8,128)}, u32[]{:S(2)}) copy-start(f32[2,16,16,8,64]{4,3,2,1,0:T(8,128)} %reshape_reshape.24) | copy-start | bytes 3145732
  454.6 78.7 %collective-permute-start.8 = (f32[2,16,1024]{2,1,0:T(8,128)}, f32[2,16,1024]{2,1,0:T(8,128)}, u32[]{:S(2)}, u32[]{:S(2)}) collective-permute-start(f32[2,16,1024]{2,1,0:T(8,128)} %get-tuple-element.101), channel_id=1, source_target_pairs={{0,1},{1,2},{2,3},{3,4},{4,5},{5,6},{6,7},{8,9},{9,10},{10,11},{11... | collective-permute-start | bytes 393224 | tf_op jit(solution)/shard_map/ppermute | solution.py:18
  457.5 82.8 %collective-permute-start.9 = (f32[2,16,1024]{2,1,0:T(8,128)}, f32[2,16,1024]{2,1,0:T(8,128)}, u32[]{:S(2)}, u32[]{:S(2)}) collective-permute-start(f32[2,16,1024]{2,1,0:T(8,128)} %get-tuple-element.100), channel_id=1, source_target_pairs={{1,0},{2,1},{3,2},{4,3},{5,4},{6,5},{7,6},{9,8},{10,9},{11,10},{12... | collective-permute-start | bytes 393224 | tf_op jit(solution)/shard_map/ppermute | solution.py:21
  472.2 15.9 %copy-start.79 = (f32[2,16,8,64]{3,2,1,0:T(8,128)S(1)}, f32[2,16,8,64]{3,2,1,0:T(8,128)}, u32[]{:S(2)}) copy-start(f32[2,16,8,64]{3,2,1,0:T(8,128)} %copy-done.78) | copy-start | bytes 196612
  472.9 56.5 %collective-permute-start.5 = (f32[2,16,1024]{2,1,0:T(8,128)}, f32[2,16,1024]{2,1,0:T(8,128)}, u32[]{:S(2)}, u32[]{:S(2)}) collective-permute-start(f32[2,16,1024]{2,1,0:T(8,128)} %maximum_bitcast_fusion), channel_id=1, source_target_pairs={{0,4},{1,5},{2,6},{3,7},{4,0},{5,1},{6,2},{7,3},{8,12},{9,13},{10,... | collective-permute-start | bytes 393224 | tf_op jit(solution)/shard_map/ppermute | solution.py:27
  533.1 5.0 collective-permute-start.6
  540.1 5.0 collective-permute-start.7
  572.6 627.5 %all-reduce.12.cloned.1.call-start = ((), (), s32[]{:S(2)}) async-start(), calls=%async_computation.1 | async-start | bytes 25165824 | tf_op jit(solution)/shard_map/psum | solution.py:322
  1002.9 50.1 %copy-start.2 = (f32[2,256,512]{2,1,0:T(8,128)S(1)}, f32[2,256,512]{2,1,0:T(8,128)}, u32[]{:S(2)}) copy-start(f32[2,256,512]{2,1,0:T(8,128)} %param.21) | copy-start | bytes 3145732
  1002.9 50.1 %copy-start.16 = (f32[512,512]{1,0:T(8,128)S(1)}, f32[512,512]{1,0:T(8,128)}, u32[]{:S(2)}) copy-start(f32[512,512]{1,0:T(8,128)} %copy-done.14) | copy-start | bytes 3145732
  1002.9 50.1 %copy-start.152 = (f32[1,2,2,128]{3,1,2,0:T(2,128)S(1)}, f32[1,2,2,128]{3,1,2,0:T(2,128)}, u32[]{:S(2)}) copy-start(f32[1,2,2,128]{3,1,2,0:T(2,128)} %copy-done.151) | copy-start | bytes 6148
  1002.9 50.1 %copy-start.154 = (f32[1,2,2,128]{3,1,2,0:T(2,128)S(1)}, f32[1,2,2,128]{3,1,2,0:T(2,128)}, u32[]{:S(2)}) copy-start(f32[1,2,2,128]{3,1,2,0:T(2,128)} %copy-done.153) | copy-start | bytes 6148
  (160 other events, 736.3 us)
Sparse Core Ops, SparseCore 0:
  572.7 401.9 all-reduce.9
  978.1 221.8 all-reduce.11
